TPU v7x, 128 devices: a whole 4x4x4 slice. The times are simulated.
128 devices in a mesh: pairs: 64 (over y, x, z), aux: 2 (over core).
Axes of the slice: x: 4, y: 4, z: 4, core: 2. Of those that a mesh axis runs over, the one named last changes fastest.
Arguments:
- densities: bfloat16 [16, 49152], P(None, 'pairs'), may hold values from -6 to 6
- tensor: bfloat16 [49152, 20480], P('pairs', 'aux'), may hold values from -0.078125 to 0.078125
- metric: bfloat16 [20480, 20480], P('aux', 'pairs'), may hold values from -0.0390625 to 0.0390625
- row_count: int32 [64], P('pairs'), may hold values from 1 to 768, 30720 in all
Outputs:
- coulomb: bfloat16 [16, 49152], P('aux', 'pairs')
Inputs may be any that keep to these rules, and one draw needn't show every extreme that they name: The first row_count[b] rows of pair block b are live; some block has all 768 rows live.
All inputs are finite; a program needn't handle non-finite values.
Results may differ from a plain program's by a relative error of at most 0.0057.
Values may be sent and summed in bfloat16 or wider, within the bound.
A program may use at most 64 MiB of HBM per device.

v0:
```python
import jax
import jax.numpy as jnp
from jax import lax
from jax.sharding import PartitionSpec as P


def cut_along(value, dim, peers):
    lengths = value.shape
    pieces = value.reshape(*lengths[:dim], peers, lengths[dim] // peers, *lengths[dim + 1 :])
    return jnp.moveaxis(pieces, dim, 0)


def sent_and_summed(value, axis, dim):
    peers = lax.axis_size(axis)
    pieces = lax.all_to_all(cut_along(value, dim, peers), axis, 0, 0, tiled=True)
    return jnp.sum(pieces, axis=0)


def sent_to_all(value, axis):
    peers = lax.axis_size(axis)
    return lax.all_to_all(
        jnp.broadcast_to(value[None], (peers, *value.shape)), axis, 0, 0, tiled=True
    )


def in_order(pieces, dim):
    pieces = jnp.moveaxis(pieces, 0, dim)
    lengths = pieces.shape
    return pieces.reshape(*lengths[:dim], lengths[dim] * lengths[dim + 1], *lengths[dim + 2 :])


def collect(value, axis, dim):
    pieces = sent_to_all(value, axis)
    return in_order(pieces, dim)


def over_pieces(value, axis):
    return lax.all_gather(value, axis).sum(0)


def body(densities, tensor, metric, row_count):
    rows_here = tensor.shape[0]
    half_aux = tensor.shape[1]
    live = lax.broadcasted_iota(jnp.int32, (1, rows_here), 1) < row_count[0]
    masked = jnp.where(live, densities, jnp.zeros_like(densities))
    fit_part = jnp.dot(masked, tensor, preferred_element_type=jnp.float32)
    shares = sent_and_summed(fit_part, "pairs", 1).astype(jnp.bfloat16)
    solved_part = jnp.dot(collect(shares, "pairs", 1), metric, preferred_element_type=jnp.float32)
    summed = over_pieces(solved_part, "aux").astype(jnp.bfloat16)
    solved = collect(summed, "pairs", 1)
    own_block = lax.dynamic_slice_in_dim(solved, lax.axis_index("aux") * half_aux, half_aux, 1)
    back_term = lax.dot_general(
        own_block, tensor, (((1,), (1,)), ((), ())), preferred_element_type=jnp.float32
    )
    returned = sent_and_summed(back_term, "aux", 0)
    return jnp.where(live, returned, jnp.zeros_like(returned)).astype(jnp.bfloat16)


def solution(mesh):
    placed = (P(None, "pairs"), P("pairs", "aux"), P("aux", "pairs"), P("pairs"))
    return jax.shard_map(
        body, mesh=mesh, in_specs=placed, out_specs=P("aux", "pairs"), check_vma=False
    )
```

profile of v0, /device:TPU:1, one launch (start us, length us, event | category | flops | bytes accessed | tf_op | source)
XLA Modules:
  0.0 102.0 jit_solution(5431501715320272648)
XLA Ops:
  0.7 7.6 %fusion.1 = f32[16,10240]{1,0:T(8,128)S(1)} fusion(bf16[768,10240]{1,0:T(8,128)(2,1)} %param.5, bf16[16,768]{1,0:T(8,128)(2,1)} %param.4, pred[768]{0:T(1024)(128)(4,1)S(1)} %iota_compare_fusion), kind=kOutput, calls=%fused_computation.4 | convolution fusion | flops 251670528 | bytes 16409344 | tf_op jit(solution)/shard_map/dot_general | solution.py:46
  8.3 0.6 reshape.23
  8.9 0.6 copy.9
  9.5 29.0 %all_to_all.20 = f32[64,16,160]{2,1,0:T(8,128)S(1)} all-to-all(f32[64,16,160]{2,1,0:T(8,128)S(1)} %bitcast.14), channel_id=1, replica_groups=mesh['pairs'=64,'aux'=2] {'pairs'}, dimensions={0} | all-to-all | bytes 1310720 | tf_op jit(solution)/shard_map/all_to_all | solution.py:15
  38.6 0.1 reduce_sum.27
  38.7 15.8 %all_to_all.21 = bf16[64,16,160]{2,1,0:T(8,128)(2,1)S(1)} all-to-all(bf16[64,16,160]{2,1,0:T(8,128)(2,1)S(1)} %broadcast_in_dim.37), channel_id=1, replica_groups=mesh['pairs'=64,'aux'=2] {'pairs'}, dimensions={0} | all-to-all | bytes 655360 | tf_op jit(solution)/shard_map/all_to_all | solution.py:21
  54.5 0.2 copy.6
  54.7 0.7 reshape.24
  55.5 4.6 %fusion.7 = f32[16,320]{1,0:T(8,128)S(1)} fusion(bf16[16,10240]{1,0:T(8,128)(2,1)S(1)} %reshape.24, bf16[10240,320]{0,1:T(8,128)(2,1)} %param.6), kind=kOutput, calls=%fused_computation.11 | convolution fusion | flops 104857600 | bytes 6901760 | tf_op jit(solution)/shard_map/dot_general | solution.py:48
  60.1 4.7 %all-gather = f32[32,320]{1,0:T(8,128)S(1)} all-gather(f32[16,320]{1,0:T(8,128)S(1)} %fusion.7), channel_id=2, replica_groups=mesh['pairs'=64,'aux'=2] {'aux'}, dimensions={0}, use_global_device_ids=true | all-gather | bytes 61440 | tf_op jit(solution)/shard_map/all_gather | solution.py:38
  64.8 0.9 broadcast_in_dim.38
  65.7 4.8 %all-to-all-start.2 = ((bf16[64,16,320]{2,1,0:T(8,128)(2,1)}), bf16[64,16,320]{2,1,0:T(8,128)(2,1)S(1)}, u32[]{:S(2)}, u32[]{:S(2)}) async-start(bf16[64,16,320]{2,1,0:T(8,128)(2,1)} %broadcast_in_dim.38), calls=%async_computation.2 | async-start | bytes 1572864 | tf_op jit(solution)/shard_map/all_to_all | solution.py:21
  70.6 14.8 %all-to-all-done.2 = bf16[64,16,320]{2,1,0:T(8,128)(2,1)S(1)} async-done(((bf16[64,16,320]{2,1,0:T(8,128)(2,1)}), bf16[64,16,320]{2,1,0:T(8,128)(2,1)S(1)}, u32[]{:S(2)}, u32[]{:S(2)}) %all-to-all-start.2) | async-done | bytes 655392 | tf_op jit(solution)/shard_map/all_to_all | solution.py:21
  85.4 0.2 copy.7
  85.6 0.8 reshape.25
  86.4 9.6 %convolution_bitcast_fusion = f32[2,8,768]{2,1,0:T(8,128)S(1)} fusion(bf16[768,10240]{1,0:T(8,128)(2,1)} %param.5, bf16[16,20480]{1,0:T(8,128)(2,1)S(1)} %reshape.25, s32[]{:T(128)S(6)} %select_n.12), kind=kOutput, calls=%fused_computation | convolution fusion | flops 251658240 | bytes 16105476 | tf_op jit(solution)/shard_map/dot_general | solution.py:52
  96.0 5.4 %all_to_all.22 = f32[2,8,768]{2,1,0:T(8,128)S(1)} all-to-all(f32[2,8,768]{2,1,0:T(8,128)S(1)} %convolution_bitcast_fusion), channel_id=1, replica_groups=mesh['pairs'=64,'aux'=2] {'aux'}, dimensions={0} | all-to-all | bytes 98304 | tf_op jit(solution)/shard_map/all_to_all | solution.py:15
  101.4 0.6 select_convert_fusion
  (4 shorter events, 0.1 us)
Async XLA Ops:
  65.7 19.7 %all-to-all-start.2 = ((bf16[64,16,320]{2,1,0:T(8,128)(2,1)}), bf16[64,16,320]{2,1,0:T(8,128)(2,1)S(1)}, u32[]{:S(2)}, u32[]{:S(2)}) async-start(bf16[64,16,320]{2,1,0:T(8,128)(2,1)} %broadcast_in_dim.38), calls=%async_computation.2 | async-start | bytes 1572864 | tf_op jit(solution)/shard_map/all_to_all | solution.py:21
where the time goes:
time: 102 us
  blocking collectives  54.9 us (54%)
  matrix products  21.9 us (21%)
  waiting for transfers between devices  14.8 us (15%)
  starting transfers between devices  4.82 us (5%)
  local copies, waits for them, and re-layouts  4.09 us (4%)
    all_to_all x2, blocking collectives, sent_and_summed(): lax.all_to_all(cut_along(value, dim, peers), axis, 0, 0, tiled=True)  34.4 us
    all_to_all x1, blocking collectives, sent_to_all(): lax.all_to_all(jnp.broadcast_to(value[None], (peers, *value.shape)), axis...  15.8 us
    all_to_all x1, waiting for transfers between devices, sent_to_all(): lax.all_to_all(jnp.broadcast_to(value[None], (peers, *value.shape)), axis...  14.8 us
    dot_general x1, matrix products, body(): lax.dot_general(own_block, tensor, (((1,), (1,)), ((), ())), preferred_el...  9.62 us
    dot_general x1, matrix products, body(): fit_part = jnp.dot(masked, tensor, preferred_element_type=jnp.float32)  7.64 us
    all_to_all x1, starting transfers between devices, sent_to_all(): lax.all_to_all(jnp.broadcast_to(value[None], (peers, *value.shape)), axis...  4.82 us
    all_gather x1, blocking collectives, over_pieces(): return lax.all_gather(value, axis).sum(0)  4.66 us
    dot_general x1, matrix products, body(): jnp.dot(collect(shares, 'pairs', 1), metric, preferred_element_type=jnp.f...  4.65 us
  transfers between devices with their start and end apart: 1, of which 1 were waited for; matrix products, arithmetic and copies ran while one was open for 0% of the time, Pallas kernels for 0%

commit v1 on v0

v1 whole, which is shorter than its diff:
```python
import functools

import jax
import jax.numpy as jnp
from jax import lax
from jax.experimental import pallas as pl
from jax.experimental.pallas import tpu as pltpu
from jax.sharding import PartitionSpec as P

MESH = pl.DeviceIdType.MESH
NT = (((1,), (1,)), ((), ()))
K, ROWS, AUX, COLS = 16, 768, 10240, 320
TILE = 128
CHUNKS = (2048, 2048, 2048, 2048, 1024, 1024)
STEPS = (2, 1, 3, 0)


def hops(step):
    return sum(min(d, 4 - d) for d in step)


OFFSETS = sorted(
    [(a, b, d) for a in STEPS for b in STEPS for d in STEPS if (a, b, d) != (0, 0, 0)],
    key=lambda step: -hops(step),
)


def tiles_of(ref, first, count):
    return jnp.concatenate([ref[first + i] for i in range(count)], axis=1)


def kernel(
    count_ref, dens_hbm, tensor_hbm, metric_hbm, out_ref,
    tv, mv, dv, fit, got, got_extra, fitted, part, solved, pieces, back, returned,
    load_d, load_t, load_m, rs_send, rs_recv, rs_recv_extra,
    ag_send, ag_recv, ag_recv_extra, c_send, c_recv, d_send, d_recv, e_send, e_recv,
):
    p, c = lax.axis_index("pairs"), lax.axis_index("aux")
    y, x, z = p // 16, (p // 4) % 4, p % 4
    group = p // 4
    has_extra = z == (x + y) % 4
    owner = p // 32

    def chip(step):
        return ((y + step[0]) % 4 * 4 + (x + step[1]) % 4) * 4 + (z + step[2]) % 4

    load_dens = pltpu.make_async_copy(dens_hbm, dv, load_d)
    load_dens.start()
    loads, at = [], 0
    for i, width in enumerate(CHUNKS):
        piece = pltpu.make_async_copy(
            tensor_hbm.at[:, pl.ds(at, width)], tv.at[:, pl.ds(at, width)], load_t.at[i]
        )
        piece.start()
        loads.append((piece, at, width))
        at += width

    barrier = pltpu.get_barrier_semaphore()
    for step in OFFSETS:
        pl.semaphore_signal(barrier, inc=1, device_id=(chip(step), c), device_id_type=MESH)
    pl.semaphore_signal(barrier, inc=1, device_id=(p, 1 - c), device_id_type=MESH)

    load_dens.wait()
    live = lax.broadcasted_iota(jnp.int32, (K, ROWS), 1) < count_ref[0]
    masked = jnp.where(live, dv[...], jnp.zeros((K, ROWS), jnp.bfloat16))
    for piece, at, width in loads:
        piece.wait()
        term = jnp.dot(masked, tv[:, at : at + width], preferred_element_type=jnp.float32)
        term = term.astype(jnp.bfloat16)
        for i in range(width // TILE):
            fit[at // TILE + i] = term[:, i * TILE : (i + 1) * TILE]

    load_metric = pltpu.make_async_copy(metric_hbm, mv, load_m)
    load_metric.start()
    pl.semaphore_wait(barrier, len(OFFSETS) + 1)

    for step in OFFSETS:
        q = chip(step)
        pltpu.make_async_remote_copy(
            fit.at[q], got.at[p], rs_send, rs_recv, device_id=(q, c), device_id_type=MESH
        ).start()

        @pl.when((q % 4) == (q // 16 + (q // 4) % 4) % 4)
        def _():
            pltpu.make_async_remote_copy(
                fit.at[64 + q // 4], got_extra.at[p], rs_send, rs_recv_extra,
                device_id=(q, c), device_id_type=MESH,
            ).start()

    got[p] = fit[p]
    pltpu.make_async_copy(got.at[pl.ds(0, 63)], got.at[pl.ds(0, 63)], rs_recv).wait()
    total = jnp.sum(got[...].astype(jnp.float32), axis=0)
    fitted[p] = total.astype(jnp.bfloat16)
    for step in OFFSETS:
        pltpu.make_async_remote_copy(
            fitted.at[p], fitted.at[p], ag_send, ag_recv.at[(4 - step[0]) % 4],
            device_id=(chip(step), c), device_id_type=MESH,
        ).start()

    @pl.when(has_extra)
    def _():
        got_extra[p] = fit[64 + group]
        pltpu.make_async_copy(
            got_extra.at[pl.ds(0, 63)], got_extra.at[pl.ds(0, 63)], rs_recv_extra
        ).wait()
        total = jnp.sum(got_extra[...].astype(jnp.float32), axis=0)
        fitted[64 + group] = total.astype(jnp.bfloat16)
        for step in OFFSETS:
            pltpu.make_async_remote_copy(
                fitted.at[64 + group], fitted.at[64 + group], ag_send,
                ag_recv_extra.at[(4 - step[0]) % 4],
                device_id=(chip(step), c), device_id_type=MESH,
            ).start()

    load_metric.wait()
    half = jnp.zeros((K, COLS), jnp.float32)
    for dy in STEPS:
        plane = (y + dy) % 4
        mains = 16 if dy else 15
        pltpu.make_async_copy(
            fitted.at[pl.ds(0, mains)], fitted.at[pl.ds(0, mains)], ag_recv.at[dy]
        ).wait()
        if dy:
            pltpu.make_async_copy(
                fitted.at[pl.ds(64, 4)], fitted.at[pl.ds(64, 4)], ag_recv_extra.at[dy]
            ).wait()
        else:
            @pl.when(has_extra)
            def _():
                pltpu.make_async_copy(
                    fitted.at[pl.ds(64, 3)], fitted.at[pl.ds(64, 3)], ag_recv_extra.at[0]
                ).wait()

            @pl.when(jnp.logical_not(has_extra))
            def _():
                pltpu.make_async_copy(
                    fitted.at[pl.ds(64, 4)], fitted.at[pl.ds(64, 4)], ag_recv_extra.at[0]
                ).wait()

        for first, many in ((plane * 16, 16), (64 + plane * 4, 4)):
            columns = pl.ds(pl.multiple_of(first * TILE, TILE), many * TILE)
            half += lax.dot_general(
                tiles_of(fitted, first, many), mv[:, columns], NT,
                preferred_element_type=jnp.float32,
            )

    send_half = pltpu.make_async_remote_copy(
        part.at[0], part.at[1], c_send, c_recv, device_id=(p, 1 - c), device_id_type=MESH
    )

    @pl.when(c != owner)
    def _():
        part[0] = half
        send_half.start()
        send_half.wait_send()

    @pl.when(c == owner)
    def _():
        send_half.wait_recv()
        whole = (half + part[1]).astype(jnp.bfloat16)
        blank = jnp.zeros((K, TILE // 2), jnp.bfloat16)
        low = jnp.concatenate([whole, blank], axis=1)
        high = jnp.concatenate([blank, whole], axis=1)
        placed = jnp.where(jnp.full(low.shape, p % 2, jnp.int32) == 0, low, high)
        mine = p - 32 * owner
        for i in range(3):
            pieces[mine, i] = placed[:, i * TILE : (i + 1) * TILE]
        for step in OFFSETS:
            pltpu.make_async_remote_copy(
                pieces.at[mine], pieces.at[mine], d_send, d_recv.at[(4 - step[1]) % 4],
                device_id=(chip(step), c), device_id_type=MESH,
            ).start()

    total = jnp.zeros((K, ROWS), jnp.float32)
    for dx in STEPS:
        column = (x + dx) % 4
        if dx:
            pltpu.make_async_copy(
                pieces.at[pl.ds(0, 8)], pieces.at[pl.ds(0, 8)], d_recv.at[dx]
            ).wait()
        else:
            for here, many in ((True, 7), (False, 8)):
                @pl.when((c == owner) == here)
                def _():
                    pltpu.make_async_copy(
                        pieces.at[pl.ds(0, many)], pieces.at[pl.ds(0, many)], d_recv.at[0]
                    ).wait()

        for plane in range(2):
            first = plane * 16 + column * 4
            row = []
            for j in (0, 2):
                row += [
                    pieces[first + j, 0],
                    pieces[first + j, 1],
                    pieces[first + j, 2] + pieces[first + j + 1, 0],
                    pieces[first + j + 1, 1],
                    pieces[first + j + 1, 2],
                ]
            columns = pl.ds(pl.multiple_of(first * COLS, TILE), 4 * COLS)
            total += lax.dot_general(
                jnp.concatenate(row, axis=1), tv[:, columns], NT,
                preferred_element_type=jnp.float32,
            )

    back[0] = total[0:8]
    back[1] = total[8:16]
    swap = pltpu.make_async_remote_copy(
        back.at[1 - c], returned, e_send, e_recv, device_id=(p, 1 - c), device_id_type=MESH
    )
    swap.start()
    swap.wait_recv()
    result = back[c] + returned[...]
    alive = lax.broadcasted_iota(jnp.int32, (8, ROWS), 1) < count_ref[0]
    out_ref[...] = jnp.where(alive, result, jnp.zeros_like(result)).astype(jnp.bfloat16)

    swap.wait_send()
    pltpu.make_async_copy(got.at[pl.ds(0, 63)], got.at[pl.ds(0, 63)], rs_send).wait()
    pltpu.make_async_copy(fitted.at[pl.ds(0, 63)], fitted.at[pl.ds(0, 63)], ag_send).wait()
    for extra, many in ((True, 15), (False, 16)):
        @pl.when(has_extra == extra)
        def _():
            pltpu.make_async_copy(
                got.at[pl.ds(0, many)], got.at[pl.ds(0, many)], rs_send
            ).wait()

    @pl.when(has_extra)
    def _():
        pltpu.make_async_copy(fitted.at[pl.ds(0, 63)], fitted.at[pl.ds(0, 63)], ag_send).wait()

    @pl.when(c == owner)
    def _():
        for many in (32, 31):
            pltpu.make_async_copy(
                pieces.at[pl.ds(0, many)], pieces.at[pl.ds(0, many)], d_send
            ).wait()


def body(densities, tensor, metric, row_count):
    anywhere = pl.BlockSpec(memory_space=pl.ANY)
    dma = pltpu.SemaphoreType.DMA
    bf16, f32 = jnp.bfloat16, jnp.float32
    return pl.pallas_call(
        kernel,
        name="coulomb",
        out_shape=jax.ShapeDtypeStruct((K // 2, ROWS), bf16),
        in_specs=[pl.BlockSpec(memory_space=pltpu.SMEM), anywhere, anywhere, anywhere],
        out_specs=pl.BlockSpec(memory_space=pltpu.VMEM),
        scratch_shapes=[
            pltpu.VMEM((ROWS, AUX), bf16),
            pltpu.VMEM((COLS, AUX), bf16),
            pltpu.VMEM((K, ROWS), bf16),
            pltpu.VMEM((80, K, TILE), bf16),
            pltpu.VMEM((64, K, TILE), bf16),
            pltpu.VMEM((64, K, TILE), bf16),
            pltpu.VMEM((80, K, TILE), bf16),
            pltpu.VMEM((2, K, COLS), f32),
            pltpu.VMEM((K, COLS), bf16),
            pltpu.VMEM((32, 3, K, TILE), bf16),
            pltpu.VMEM((2, K // 2, ROWS), f32),
            pltpu.VMEM((K // 2, ROWS), f32),
            dma, dma((len(CHUNKS),)), dma, dma, dma, dma,
            dma, dma((4,)), dma((4,)), dma, dma, dma, dma((4,)), dma, dma,
        ],
        compiler_params=pltpu.CompilerParams(
            collective_id=0, has_side_effects=True, vmem_limit_bytes=56 << 20
        ),
    )(row_count, densities, tensor, metric.T)


def solution(mesh):
    placed = (P(None, "pairs"), P("pairs", "aux"), P("aux", "pairs"), P("pairs"))
    return jax.shard_map(
        body, mesh=mesh, in_specs=placed, out_specs=P("aux", "pairs"), check_vma=False
    )
```

time: 102 us -> 51.1 us (0.50)
  blocking collectives: 54.9 us -> 0 us
  Pallas kernels: 0 us -> 49 us
  matrix products: 21.9 us -> 0 us
  waiting for transfers between devices: 14.8 us -> 0 us
  starting transfers between devices: 4.82 us -> 0 us
  local copies, waits for them, and re-layouts: 4.09 us -> 1.31 us
    all_to_all x3 -> x0, blocking collectives: 50.2 us -> none  [the longest x2 34.4 us: sent_and_summed(): lax.all_to_all(cut_along(value, dim, peers), axis, 0, 0, tiled=True)]
    pallas_call x0 -> x1, Pallas kernels: none -> 49 us  [body(): pl.pallas_call(kernel, name='coulomb', out_shape=jax.ShapeDtypeStruct((K...]
    dot_general x3 -> x0, matrix products: 21.9 us -> none  [the longest x1 9.62 us: body(): lax.dot_general(own_block, tensor, (((1,), (1,)), ((), ())), preferred_el...]
    all_to_all x1 -> x0, waiting for transfers between devices: 14.8 us -> none  [sent_to_all(): lax.all_to_all(jnp.broadcast_to(value[None], (peers, *value.shape)), axis...]
    all_to_all x1 -> x0, starting transfers between devices: 4.82 us -> none  [sent_to_all(): lax.all_to_all(jnp.broadcast_to(value[None], (peers, *value.shape)), axis...]
    all_gather x1 -> x0, blocking collectives: 4.66 us -> none  [over_pieces(): return lax.all_gather(value, axis).sum(0)]
    reshape x4 -> x0, local copies, waits for them, and re-layouts: 2.76 us -> none  [the longest x2 1.57 us: in_order(): pieces.reshape(*lengths[:dim], lengths[dim] * lengths[dim + 1], *lengths[...]
    unnamed x0 -> x1, local copies, waits for them, and re-layouts: none -> 1.31 us
  transfers between devices with their start and end apart: 1 -> 0, of which waited for: 1 -> 0; matrix products, arithmetic and copies ran while one was open for 0% -> 0% of each run, Pallas kernels for 0% -> 0%
where the time goes in v1:
time: 51.1 us; the launch traced here: 51 us
  Pallas kernels  49 us (96%)
  local copies, waits for them, and re-layouts  1.31 us (3%)
  between operations  0.66 us (1%)
    pallas_call x1, Pallas kernels, body(): pl.pallas_call(kernel, name='coulomb', out_shape=jax.ShapeDtypeStruct((K...  49 us
    unnamed x1, local copies, waits for them, and re-layouts  1.31 us

profile of v1, /device:TPU:1, one launch (start us, length us, event | category | flops | bytes accessed | tf_op | source)
XLA Modules:
  0.0 51.0 jit_solution(5132012777351058371)
XLA Ops:
  0.7 49.0 %coulomb.1 = bf16[8,768]{1,0:T(8,128)(2,1)} custom-call(s32[1]{0:T(128)S(6)} %copy.6.count_ref, bf16[16,768]{1,0:T(8,128)(2,1)} %dens_hbm.1, bf16[768,10240]{1,0:T(8,128)(2,1)} %tensor_hbm.1, bf16[320,10240]{1,0:T(8,128)(2,1)} %bitcast.1), custom_call_target="tpu_custom_call" | custom-call | tf_op jit(solution)/shard_map/coulomb/pallas_call | solution.py:243
  49.7 1.3 %copy.7 = bf16[8,768]{1,0:T(8,128)(2,1)} copy(bf16[8,768]{1,0:T(8,128)(2,1)} %coulomb.1) | data formatting | bytes 24576

commit v2 on v0

v2 whole, which is shorter than its diff:
```python
import jax
import jax.numpy as jnp
from jax import lax
from jax.experimental import pallas as pl
from jax.experimental.pallas import tpu as pltpu
from jax.sharding import PartitionSpec as P

MESH = pl.DeviceIdType.MESH
K, ROWS, AUX, COLS = 16, 768, 10240, 320
TILE, WIDTH, PLANE = 128, 1024, 2048
FLYING = 6
GATE = 2
TURN = 512
EARLY = 12


def nth(a):
    return (2 + 3 * a + 3 * (a * (a - 1) // 2)) % 4


def total_of(terms):
    while len(terms) > 1:
        terms = [sum(terms[i + 1 : i + 2], terms[i]) for i in range(0, len(terms), 2)]
    return terms[0]


def repeat(count, what):
    def one(i, carry):
        what(i)
        return carry

    lax.fori_loop(0, count, one, 0)


def kernel(
    count_hbm, dens_hbm, tensor_hbm, metric_hbm, out_ref,
    count, tv, mv, tt, mt, dv, fit, got, stage, fitted, part, piece, pieces, back, returned,
    load_n, load_d, load_t, load_m, rs_send, rs_recv,
    ag_send, ag_recv, c_send, c_recv, d_send, d_recv, e_send, e_recv,
):
    p, c = lax.axis_index("pairs"), lax.axis_index("aux")
    y, x, z = p // 16, (p // 4) % 4, p % 4
    diagonal = (x + y + z) % 4
    has_extra = diagonal == 0
    owner = p // 32
    mine = p - 32 * owner

    def chip(dy, dx, dz):
        return ((y + dy) % 4 * 4 + (x + dx) % 4) * 4 + (z + dz) % 4

    def to_all(order, act):
        def row(i):
            first, second = nth(i // 4), nth(i % 4)
            for dz in (2, 1, 3):
                act(*order(first, second), dz)

            @pl.when(i != 15)
            def _():
                act(*order(first, second), 0)

        repeat(16, row)

    load_dens = pltpu.make_async_copy(dens_hbm, dv, load_d)
    load_dens.start()
    load_count = pltpu.make_async_copy(count_hbm, count, load_n)
    load_count.start()

    def plane_of(n):
        return (y + nth(n - 1)) % 4

    def columns_of(m):
        n = m // 2
        is_main = (n + 4) // 5
        first = is_main * plane_of(n) * PLANE + (1 - is_main) * 64 * TILE + (m % 2) * WIDTH
        return pl.ds(pl.multiple_of(first, WIDTH), WIDTH)

    def load(m):
        columns = columns_of(m)
        return pltpu.make_async_copy(tensor_hbm.at[:, columns], tv.at[:, columns], load_t.at[m])

    repeat(FLYING, lambda m: load(m).start())
    load_metric = pltpu.make_async_copy(metric_hbm, mv, load_m)

    barrier = pltpu.get_barrier_semaphore()
    to_all(
        lambda a, b: (a, b),
        lambda dy, dx, dz: pl.semaphore_signal(
            barrier, inc=1, device_id=(chip(dy, dx, dz), c), device_id_type=MESH
        ),
    )
    pl.semaphore_signal(barrier, inc=1, device_id=(p, 1 - c), device_id_type=MESH)

    load_count.wait()
    load_dens.wait()
    live = lax.broadcasted_iota(jnp.int32, (K, ROWS), 1) < count[0]
    dv[...] = jnp.where(live, dv[...], jnp.zeros((K, ROWS), jnp.bfloat16))

    def send_plane(n, carry):
        dy = nth(n - 1)

        def row(i):
            dx = nth(i)
            for dz in (2, 1, 3, 0):
                q = chip(dy, dx, dz)
                elsewhere = True if dz else (n != 4) | (i != 3)
                extra = (diagonal + dy + dx + dz) % 4 == 0
                for many in (2, 1):
                    @pl.when((extra == (many == 2)) & elsewhere)
                    def _():
                        pltpu.make_async_remote_copy(
                            fit.at[pl.ds(2 * q, many)], got.at[pl.ds(2 * p, many)],
                            rs_send, rs_recv, device_id=(q, c), device_id_type=MESH,
                        ).start()

        repeat(4, row)
        return carry

    def fit_step(m):
        n = m // 2
        is_main = (n + 4) // 5
        load(m).wait()

        @pl.when(m + FLYING < AUX // WIDTH)
        def _():
            load(m + FLYING).start()

        @pl.when(m + FLYING == AUX // WIDTH)
        def _():
            load_metric.start()

        term = jnp.dot(dv[...], tv[:, columns_of(m)], preferred_element_type=jnp.float32)
        term = term.astype(jnp.bfloat16)
        for j in range(WIDTH // TILE):
            tile = (m % 2) * (WIDTH // TILE) + j
            extra = 2 * (4 * tile + (12 - tile // 4 - tile % 4) % 4) + 1
            slot = is_main * 2 * (plane_of(n) * 16 + tile) + (1 - is_main) * extra
            fit[slot] = term[:, j * TILE : (j + 1) * TILE]

        @pl.when(m == 2 * GATE + 1)
        def _():
            pl.semaphore_wait(barrier, 64)

        @pl.when((m % 2 == 1) & (n >= GATE))
        def _():
            lax.fori_loop(1 + (n - GATE + 3) // 4 * (n - 1), n + 1, send_plane, 0)

    repeat(AUX // WIDTH, fit_step)
    def turn(source, target):
        def one(i, carry):
            columns = pl.ds(pl.multiple_of(i * TURN, TURN), TURN)
            target[columns, :] = source[:, columns].T
            return carry

        return one

    for many in (2, 1):
        @pl.when(has_extra == (many == 2))
        def _():
            own = pl.ds(2 * p, many)
            pltpu.make_async_copy(fit.at[own], got.at[own], rs_recv).start()

    if EARLY:
        lax.fori_loop(0, EARLY, turn(tv, tt), 0)
    for many in (2, 1):
        @pl.when(has_extra == (many == 2))
        def _():
            everything = got.at[pl.ds(0, 64 * many)]
            pltpu.make_async_copy(everything, everything, rs_recv).wait()
            for i in range(many):
                total = total_of([got[2 * q + i].astype(jnp.float32) for q in range(64)])
                stage[i] = total.astype(jnp.bfloat16)
            share, place = stage.at[pl.ds(0, many)], fitted.at[pl.ds(2 * p, many)]
            to_all(
                lambda a, b: (a, b),
                lambda dy, dx, dz: pltpu.make_async_remote_copy(
                    share, place, ag_send, ag_recv.at[(4 - dy) % 4],
                    device_id=(chip(dy, dx, dz), c), device_id_type=MESH,
                ).start(),
            )
            pltpu.make_async_copy(share, place, ag_recv.at[0]).start()

    load_metric.wait()
    lax.fori_loop(0, AUX // TURN, turn(mv, mt), 0)
    lax.fori_loop(EARLY, AUX // TURN, turn(tv, tt), 0)

    def solve(a, half):
        dy = nth(a)
        plane = (y + dy) % 4
        arrived = fitted.at[pl.ds(0, 20)]
        pltpu.make_async_copy(arrived, arrived, ag_recv.at[dy]).wait()
        slots = [2 * (plane * 16 + i) for i in range(16)]
        extras = [2 * (plane * 16 + 4 * j + (12 - plane - j) % 4) + 1 for j in range(4)]
        for first, here in ((plane * 16, slots), (64 + plane * 4, extras)):
            rows = pl.ds(pl.multiple_of(first * TILE, 4 * TILE), len(here) * TILE)
            half += jnp.dot(
                jnp.concatenate([fitted[slot] for slot in here], axis=1), mt[rows, :],
                preferred_element_type=jnp.float32,
            )
        return half

    part[0] = lax.fori_loop(0, 4, solve, jnp.zeros((K, COLS), jnp.float32))

    exchange = pltpu.make_async_remote_copy(
        part.at[0], part.at[1], c_send, c_recv, device_id=(p, 1 - c), device_id_type=MESH
    )

    @pl.when(c != owner)
    def _():
        exchange.start()
        exchange.wait_send()

    @pl.when(c == owner)
    def _():
        exchange.wait_recv()
        whole = (part[0] + part[1]).astype(jnp.bfloat16)
        blank = jnp.zeros((K, TILE // 2), jnp.bfloat16)
        low = jnp.concatenate([whole, blank], axis=1)
        high = jnp.concatenate([blank, whole], axis=1)
        placed = jnp.where(jnp.full(low.shape, p % 2, jnp.int32) == 0, low, high)
        for i in range(3):
            piece[i] = placed[:, i * TILE : (i + 1) * TILE]
        to_all(
            lambda a, b: (b, a),
            lambda dy, dx, dz: pltpu.make_async_remote_copy(
                piece, pieces.at[mine], d_send, d_recv.at[(4 - dx) % 4],
                device_id=(chip(dy, dx, dz), c), device_id_type=MESH,
            ).start(),
        )
        pltpu.make_async_copy(piece, pieces.at[mine], d_recv.at[0]).start()

    def back_step(i, total):
        dx = nth(i // 2)
        first = i % 2 * 16 + (x + dx) % 4 * 4

        @pl.when(i % 2 == 0)
        def _():
            arrived = pieces.at[pl.ds(0, 8)]
            pltpu.make_async_copy(arrived, arrived, d_recv.at[dx]).wait()

        row = []
        for j in (0, 2):
            row += [
                pieces[first + j, 0],
                pieces[first + j, 1],
                pieces[first + j, 2] + pieces[first + j + 1, 0],
                pieces[first + j + 1, 1],
                pieces[first + j + 1, 2],
            ]
        rows = pl.ds(pl.multiple_of(first * COLS, 4 * COLS), 4 * COLS)
        return total + jnp.dot(
            jnp.concatenate(row, axis=1), tt[rows, :], preferred_element_type=jnp.float32
        )

    total = lax.fori_loop(0, 8, back_step, jnp.zeros((K, ROWS), jnp.float32))
    back[0] = total[0:8]
    back[1] = total[8:16]
    result = back[c]

    swap = pltpu.make_async_remote_copy(
        back.at[1 - c], returned, e_send, e_recv, device_id=(p, 1 - c), device_id_type=MESH
    )
    swap.start()
    swap.wait_recv()
    result = back[c] + returned[...]
    swap.wait_send()
    alive = lax.broadcasted_iota(jnp.int32, (K // 2, ROWS), 1) < count[0]
    out_ref[...] = jnp.where(alive, result, jnp.zeros_like(result))

    for extra in (True, False):
        @pl.when(has_extra == extra)
        def _():
            sent = fit.at[pl.ds(0, 78 if extra else 79)]
            pltpu.make_async_copy(sent, sent, rs_send).wait()
            sent = fitted.at[pl.ds(0, 126 if extra else 63)]
            pltpu.make_async_copy(sent, sent, ag_send).wait()

    @pl.when(c == owner)
    def _():
        for many in (32, 31):
            sent = pieces.at[pl.ds(0, many)]
            pltpu.make_async_copy(sent, sent, d_send).wait()


def body(densities, tensor, metric, row_count):
    hbm = pl.BlockSpec(memory_space=pltpu.HBM)
    dma = pltpu.SemaphoreType.DMA
    bf16, f32 = jnp.bfloat16, jnp.float32
    out = pl.pallas_call(
        kernel,
        name="coulomb",
        out_shape=pltpu.VMEM((K // 2, ROWS), f32),
        in_specs=[hbm, hbm, hbm, hbm],
        out_specs=pl.BlockSpec(memory_space=pltpu.VMEM),
        scratch_shapes=[
            pltpu.SMEM((1,), jnp.int32),
            pltpu.VMEM((ROWS, AUX), bf16),
            pltpu.VMEM((COLS, AUX), bf16),
            pltpu.VMEM((AUX, ROWS), bf16),
            pltpu.VMEM((AUX, COLS), bf16),
            pltpu.VMEM((K, ROWS), bf16),
            pltpu.VMEM((128, K, TILE), bf16),
            pltpu.VMEM((128, K, TILE), bf16),
            pltpu.VMEM((2, K, TILE), bf16),
            pltpu.VMEM((128, K, TILE), bf16),
            pltpu.VMEM((2, K, COLS), f32),
            pltpu.VMEM((3, K, TILE), bf16),
            pltpu.VMEM((32, 3, K, TILE), bf16),
            pltpu.VMEM((2, K // 2, ROWS), f32),
            pltpu.VMEM((K // 2, ROWS), f32),
            dma, dma, dma((AUX // WIDTH,)), dma, dma, dma,
            dma, dma((4,)), dma, dma, dma, dma((4,)), dma, dma,
        ],
        compiler_params=pltpu.CompilerParams(
            collective_id=0, has_side_effects=True, vmem_limit_bytes=54 << 20
        ),
    )(row_count, densities, tensor, metric.T)
    return out.astype(bf16)


def solution(mesh):
    placed = (P(None, "pairs"), P("pairs", "aux"), P("aux", "pairs"), P("pairs"))
    return jax.shard_map(
        body, mesh=mesh, in_specs=placed, out_specs=P("aux", "pairs"), check_vma=False
    )
```

time: 102 us -> 41.5 us (0.41)
  blocking collectives: 54.9 us -> 0 us
  Pallas kernels: 0 us -> 40.1 us
  matrix products: 21.9 us -> 0 us
  waiting for transfers between devices: 14.8 us -> 0 us
  starting transfers between devices: 4.82 us -> 0 us
  local copies, waits for them, and re-layouts: 4.09 us -> 0 us
    all_to_all x3 -> x0, blocking collectives: 50.2 us -> none  [the longest x2 34.4 us: sent_and_summed(): lax.all_to_all(cut_along(value, dim, peers), axis, 0, 0, tiled=True)]
    pallas_call x0 -> x1, Pallas kernels: none -> 40.1 us  [body(): pl.pallas_call(kernel, name='coulomb', out_shape=pltpu.VMEM((K // 2, ROWS...]
    dot_general x3 -> x0, matrix products: 21.9 us -> none  [the longest x1 9.62 us: body(): lax.dot_general(own_block, tensor, (((1,), (1,)), ((), ())), preferred_el...]
    all_to_all x1 -> x0, waiting for transfers between devices: 14.8 us -> none  [sent_to_all(): lax.all_to_all(jnp.broadcast_to(value[None], (peers, *value.shape)), axis...]
    all_to_all x1 -> x0, starting transfers between devices: 4.82 us -> none  [sent_to_all(): lax.all_to_all(jnp.broadcast_to(value[None], (peers, *value.shape)), axis...]
    all_gather x1 -> x0, blocking collectives: 4.66 us -> none  [over_pieces(): return lax.all_gather(value, axis).sum(0)]
    reshape x4 -> x0, local copies, waits for them, and re-layouts: 2.76 us -> none  [the longest x2 1.57 us: in_order(): pieces.reshape(*lengths[:dim], lengths[dim] * lengths[dim + 1], *lengths[...]
  transfers between devices with their start and end apart: 1 -> 0, of which waited for: 1 -> 0; matrix products, arithmetic and copies ran while one was open for 0% -> 0% of each run, Pallas kernels for 0% -> 0%
where the time goes in v2:
time: 41.5 us; the launch traced here: 41.4 us
  Pallas kernels  40.1 us (97%)
  between operations  0.66 us (2%)
  other arithmetic  0.6 us (1%)
    pallas_call x1, Pallas kernels, body(): pl.pallas_call(kernel, name='coulomb', out_shape=pltpu.VMEM((K // 2, ROWS...  40.1 us

profile of v2, /device:TPU:1, one launch (start us, length us, event | category | flops | bytes accessed | tf_op | source)
XLA Modules:
  0.0 41.4 jit_solution(10174004327287132868)
XLA Ops:
  0.7 40.1 %coulomb.1 = f32[8,768]{1,0:T(8,128)S(1)} custom-call(s32[1]{0:T(128)S(6)} %copy.5.count_hbm, bf16[16,768]{1,0:T(8,128)(2,1)} %dens_hbm.1, bf16[768,10240]{1,0:T(8,128)(2,1)} %tensor_hbm.1, bf16[320,10240]{1,0:T(8,128)(2,1)} %bitcast.1), custom_call_target="tpu_custom_call" | custom-call | tf_op jit(solution)/shard_map/coulomb/pallas_call | solution.py:288
  40.8 0.6 %convert_element_type.3 = bf16[8,768]{1,0:T(8,128)(2,1)} convert(f32[8,768]{1,0:T(8,128)S(1)} %coulomb.1) | non-fusion elementwise | flops 6144 | bytes 36864 | tf_op jit(solution)/shard_map/convert_element_type | solution.py:317

commit v3 on v2

--- a/solution.py
+++ b/solution.py
@@ -8,14 +8,19 @@
 MESH = pl.DeviceIdType.MESH
 K, ROWS, AUX, COLS = 16, 768, 10240, 320
 TILE, WIDTH, PLANE = 128, 1024, 2048
-FLYING = 6
 GATE = 2
 TURN = 512
 EARLY = 12
+FIRST = 3
+FLYING = 6
 
 
 def nth(a):
     return (2 + 3 * a + 3 * (a * (a - 1) // 2)) % 4
+
+
+def near(a):
+    return (a + a * (a - 1) // 2) % 4
 
 
 def total_of(terms):
@@ -48,17 +53,19 @@
     def chip(dy, dx, dz):
         return ((y + dy) % 4 * 4 + (x + dx) % 4) * 4 + (z + dz) % 4
 
-    def to_all(order, act):
-        def row(i):
-            first, second = nth(i // 4), nth(i % 4)
-            for dz in (2, 1, 3):
-                act(*order(first, second), dz)
-
-            @pl.when(i != 15)
-            def _():
-                act(*order(first, second), 0)
-
-        repeat(16, row)
+    def to_all(order, act, outer=nth):
+        def block(i):
+            first = outer(i)
+            for second in (2, 1, 3, 0):
+                for dz in (2, 1, 3, 0):
+                    if second or dz:
+                        act(*order(first, second), dz)
+                    else:
+                        @pl.when(first != 0)
+                        def _():
+                            act(*order(first, second), dz)
+
+        repeat(4, block)
 
     load_dens = pltpu.make_async_copy(dens_hbm, dv, load_d)
     load_dens.start()
@@ -78,9 +85,7 @@
         columns = columns_of(m)
         return pltpu.make_async_copy(tensor_hbm.at[:, columns], tv.at[:, columns], load_t.at[m])
 
-    repeat(FLYING, lambda m: load(m).start())
-    load_metric = pltpu.make_async_copy(metric_hbm, mv, load_m)
-
+    repeat(FIRST, lambda m: load(m).start())
     barrier = pltpu.get_barrier_semaphore()
     to_all(
         lambda a, b: (a, b),
@@ -90,29 +95,43 @@
     )
     pl.semaphore_signal(barrier, inc=1, device_id=(p, 1 - c), device_id_type=MESH)
 
+    lax.fori_loop(FIRST, FLYING, lambda m, carry: (load(m).start(), carry)[1], 0)
+    load_metric = pltpu.make_async_copy(metric_hbm, mv, load_m)
+
     load_count.wait()
     load_dens.wait()
     live = lax.broadcasted_iota(jnp.int32, (K, ROWS), 1) < count[0]
     dv[...] = jnp.where(live, dv[...], jnp.zeros((K, ROWS), jnp.bfloat16))
 
+    def send_fit(dy, dx, dz, many):
+        q = chip(dy, dx, dz)
+        pltpu.make_async_remote_copy(
+            fit.at[pl.ds(2 * q, many)], got.at[pl.ds(2 * p, many)],
+            rs_send, rs_recv, device_id=(q, c), device_id_type=MESH,
+        ).start()
+
     def send_plane(n, carry):
         dy = nth(n - 1)
-
-        def row(i):
-            dx = nth(i)
-            for dz in (2, 1, 3, 0):
-                q = chip(dy, dx, dz)
-                elsewhere = True if dz else (n != 4) | (i != 3)
-                extra = (diagonal + dy + dx + dz) % 4 == 0
+        lead = 16 - diagonal - dy
+
+        def row(dx):
+            for dz, many in ((0, 2), (2, 1), (1, 1), (3, 1)):
+                send_fit(dy, dx, lead - dx + dz, many)
+
+        for dx in (2, 1, 3):
+            row(dx)
+        @pl.when(dy != 0)
+        def _():
+            row(0)
+
+        @pl.when(dy == 0)
+        def _():
+            for dz in (2, 1, 3):
                 for many in (2, 1):
-                    @pl.when((extra == (many == 2)) & elsewhere)
+                    @pl.when(((diagonal + dz) % 4 == 0) == (many == 2))
                     def _():
-                        pltpu.make_async_remote_copy(
-                            fit.at[pl.ds(2 * q, many)], got.at[pl.ds(2 * p, many)],
-                            rs_send, rs_recv, device_id=(q, c), device_id_type=MESH,
-                        ).start()
-
-        repeat(4, row)
+                        send_fit(0, 0, dz, many)
+
         return carry
 
     def fit_step(m):
@@ -123,10 +142,6 @@
         @pl.when(m + FLYING < AUX // WIDTH)
         def _():
             load(m + FLYING).start()
-
-        @pl.when(m + FLYING == AUX // WIDTH)
-        def _():
-            load_metric.start()
 
         term = jnp.dot(dv[...], tv[:, columns_of(m)], preferred_element_type=jnp.float32)
         term = term.astype(jnp.bfloat16)
@@ -145,6 +160,7 @@
             lax.fori_loop(1 + (n - GATE + 3) // 4 * (n - 1), n + 1, send_plane, 0)
 
     repeat(AUX // WIDTH, fit_step)
+    load_metric.start()
     def turn(source, target):
         def one(i, carry):
             columns = pl.ds(pl.multiple_of(i * TURN, TURN), TURN)
@@ -159,8 +175,7 @@
             own = pl.ds(2 * p, many)
             pltpu.make_async_copy(fit.at[own], got.at[own], rs_recv).start()
 
-    if EARLY:
-        lax.fori_loop(0, EARLY, turn(tv, tt), 0)
+    lax.fori_loop(0, EARLY, turn(tv, tt), 0)
     for many in (2, 1):
         @pl.when(has_extra == (many == 2))
         def _():
@@ -175,7 +190,7 @@
                 lambda dy, dx, dz: pltpu.make_async_remote_copy(
                     share, place, ag_send, ag_recv.at[(4 - dy) % 4],
                     device_id=(chip(dy, dx, dz), c), device_id_type=MESH,
-                ).start(),
+                ).start(), nth,
             )
             pltpu.make_async_copy(share, place, ag_recv.at[0]).start()
 
@@ -212,24 +227,29 @@
     @pl.when(c == owner)
     def _():
         exchange.wait_recv()
-        whole = (part[0] + part[1]).astype(jnp.bfloat16)
-        blank = jnp.zeros((K, TILE // 2), jnp.bfloat16)
-        low = jnp.concatenate([whole, blank], axis=1)
-        high = jnp.concatenate([blank, whole], axis=1)
-        placed = jnp.where(jnp.full(low.shape, p % 2, jnp.int32) == 0, low, high)
-        for i in range(3):
-            piece[i] = placed[:, i * TILE : (i + 1) * TILE]
+        whole = part[0] + part[1]
+        even = jnp.full((K, 2 * TILE), p % 2, jnp.int32) == 0
+        full = jnp.where(even, whole[:, 0 : 2 * TILE], whole[:, TILE // 2 : COLS])
+        rest = jnp.where(
+            even[:, 0 : TILE // 2], whole[:, 2 * TILE : COLS], whole[:, 0 : TILE // 2]
+        )
+        both = jnp.concatenate([rest[0:8], rest[8:16]], axis=1)
+        for i, half_tile in enumerate((
+            full[0:8, 0:TILE], full[8:16, 0:TILE],
+            full[0:8, TILE:], full[8:16, TILE:], both,
+        )):
+            piece[i] = half_tile.astype(jnp.bfloat16)
         to_all(
             lambda a, b: (b, a),
             lambda dy, dx, dz: pltpu.make_async_remote_copy(
                 piece, pieces.at[mine], d_send, d_recv.at[(4 - dx) % 4],
                 device_id=(chip(dy, dx, dz), c), device_id_type=MESH,
-            ).start(),
+            ).start(), near,
         )
         pltpu.make_async_copy(piece, pieces.at[mine], d_recv.at[0]).start()
 
     def back_step(i, total):
-        dx = nth(i // 2)
+        dx = near(i // 2)
         first = i % 2 * 16 + (x + dx) % 4 * 4
 
         @pl.when(i % 2 == 0)
@@ -237,15 +257,21 @@
             arrived = pieces.at[pl.ds(0, 8)]
             pltpu.make_async_copy(arrived, arrived, d_recv.at[dx]).wait()
 
-        row = []
+        upper, lower = [], []
         for j in (0, 2):
-            row += [
-                pieces[first + j, 0],
-                pieces[first + j, 1],
-                pieces[first + j, 2] + pieces[first + j + 1, 0],
-                pieces[first + j + 1, 1],
-                pieces[first + j + 1, 2],
+            left, right = pieces[first + j, 4], pieces[first + j + 1, 4]
+            middle = TILE // 2
+            upper += [
+                pieces[first + j, 0], pieces[first + j, 2],
+                jnp.concatenate([left[:, :middle], right[:, :middle]], axis=1),
+                pieces[first + j + 1, 0], pieces[first + j + 1, 2],
             ]
+            lower += [
+                pieces[first + j, 1], pieces[first + j, 3],
+                jnp.concatenate([left[:, middle:], right[:, middle:]], axis=1),
+                pieces[first + j + 1, 1], pieces[first + j + 1, 3],
+            ]
+        row = [jnp.concatenate(pair, axis=0) for pair in zip(upper, lower)]
         rows = pl.ds(pl.multiple_of(first * COLS, 4 * COLS), 4 * COLS)
         return total + jnp.dot(
             jnp.concatenate(row, axis=1), tt[rows, :], preferred_element_type=jnp.float32
@@ -303,8 +329,8 @@
             pltpu.VMEM((2, K, TILE), bf16),
             pltpu.VMEM((128, K, TILE), bf16),
             pltpu.VMEM((2, K, COLS), f32),
-            pltpu.VMEM((3, K, TILE), bf16),
-            pltpu.VMEM((32, 3, K, TILE), bf16),
+            pltpu.VMEM((5, 8, TILE), bf16),
+            pltpu.VMEM((32, 5, 8, TILE), bf16),
             pltpu.VMEM((2, K // 2, ROWS), f32),
             pltpu.VMEM((K // 2, ROWS), f32),
             dma, dma, dma((AUX // WIDTH,)), dma, dma, dma,

time: 41.5 us -> 39.5 us (0.952)
  Pallas kernels: 40.1 us -> 38.1 us
    pallas_call x1, Pallas kernels: 40.1 us -> 38.1 us  [body(): pl.pallas_call(kernel, name='coulomb', out_shape=pltpu.VMEM((K // 2, ROWS...]
where the time goes in v3:
time: 39.5 us; the launch traced here: 39.4 us
  Pallas kernels  38.1 us (96%)
  between operations  0.66 us (2%)
  other arithmetic  0.6 us (2%)
    pallas_call x1, Pallas kernels, body(): pl.pallas_call(kernel, name='coulomb', out_shape=pltpu.VMEM((K // 2, ROWS...  38.1 us

profile of v3, /device:TPU:1, one launch (start us, length us, event | category | flops | bytes accessed | tf_op | source)
XLA Modules:
  0.0 39.4 jit_solution(15548728496754109885)
XLA Ops:
  0.7 38.1 %coulomb.1 = f32[8,768]{1,0:T(8,128)S(1)} custom-call(s32[1]{0:T(128)S(6)} %copy.5.count_hbm, bf16[16,768]{1,0:T(8,128)(2,1)} %dens_hbm.1, bf16[768,10240]{1,0:T(8,128)(2,1)} %tensor_hbm.1, bf16[320,10240]{1,0:T(8,128)(2,1)} %bitcast.1), custom_call_target="tpu_custom_call" | custom-call | tf_op jit(solution)/shard_map/coulomb/pallas_call | solution.py:314
  38.8 0.6 %convert_element_type.3 = bf16[8,768]{1,0:T(8,128)(2,1)} convert(f32[8,768]{1,0:T(8,128)S(1)} %coulomb.1) | non-fusion elementwise | flops 6144 | bytes 36864 | tf_op jit(solution)/shard_map/convert_element_type | solution.py:343

commit v4 on v3

--- a/solution.py
+++ b/solution.py
@@ -45,7 +45,7 @@
 ):
     p, c = lax.axis_index("pairs"), lax.axis_index("aux")
     y, x, z = p // 16, (p // 4) % 4, p % 4
-    diagonal = (x + y + z) % 4
+    diagonal = (x + y + z + 2 * c) % 4
     has_extra = diagonal == 0
     owner = p // 32
     mine = p - 32 * owner
@@ -147,7 +147,7 @@
         term = term.astype(jnp.bfloat16)
         for j in range(WIDTH // TILE):
             tile = (m % 2) * (WIDTH // TILE) + j
-            extra = 2 * (4 * tile + (12 - tile // 4 - tile % 4) % 4) + 1
+            extra = 2 * (4 * tile + (12 - tile // 4 - tile % 4 - 2 * c) % 4) + 1
             slot = is_main * 2 * (plane_of(n) * 16 + tile) + (1 - is_main) * extra
             fit[slot] = term[:, j * TILE : (j + 1) * TILE]
 
@@ -204,7 +204,7 @@
         arrived = fitted.at[pl.ds(0, 20)]
         pltpu.make_async_copy(arrived, arrived, ag_recv.at[dy]).wait()
         slots = [2 * (plane * 16 + i) for i in range(16)]
-        extras = [2 * (plane * 16 + 4 * j + (12 - plane - j) % 4) + 1 for j in range(4)]
+        extras = [2 * (plane * 16 + 4 * j + (12 - plane - j - 2 * c) % 4) + 1 for j in range(4)]
         for first, here in ((plane * 16, slots), (64 + plane * 4, extras)):
             rows = pl.ds(pl.multiple_of(first * TILE, 4 * TILE), len(here) * TILE)
             half += jnp.dot(

time: 39.5 us -> 38.1 us (0.965)
  Pallas kernels: 38.1 us -> 36.8 us
    pallas_call x1, Pallas kernels: 38.1 us -> 36.8 us  [body(): pl.pallas_call(kernel, name='coulomb', out_shape=pltpu.VMEM((K // 2, ROWS...]
where the time goes in v4:
time: 38.1 us; the launch traced here: 38 us
  Pallas kernels  36.8 us (97%)
  between operations  0.66 us (2%)
  other arithmetic  0.6 us (2%)
    pallas_call x1, Pallas kernels, body(): pl.pallas_call(kernel, name='coulomb', out_shape=pltpu.VMEM((K // 2, ROWS...  36.8 us

profile of v4, /device:TPU:1, one launch (start us, length us, event | category | flops | bytes accessed | tf_op | source)
XLA Modules:
  0.0 38.0 jit_solution(12865021696428548812)
XLA Ops:
  0.7 36.8 %coulomb.1 = f32[8,768]{1,0:T(8,128)S(1)} custom-call(s32[1]{0:T(128)S(6)} %copy.5.count_hbm, bf16[16,768]{1,0:T(8,128)(2,1)} %dens_hbm.1, bf16[768,10240]{1,0:T(8,128)(2,1)} %tensor_hbm.1, bf16[320,10240]{1,0:T(8,128)(2,1)} %bitcast.1), custom_call_target="tpu_custom_call" | custom-call | tf_op jit(solution)/shard_map/coulomb/pallas_call | solution.py:314
  37.4 0.6 %convert_element_type.3 = bf16[8,768]{1,0:T(8,128)(2,1)} convert(f32[8,768]{1,0:T(8,128)S(1)} %coulomb.1) | non-fusion elementwise | flops 6144 | bytes 36864 | tf_op jit(solution)/shard_map/convert_element_type | solution.py:343

commit v5 on v4

--- a/solution.py
+++ b/solution.py
@@ -67,11 +67,6 @@
 
         repeat(4, block)
 
-    load_dens = pltpu.make_async_copy(dens_hbm, dv, load_d)
-    load_dens.start()
-    load_count = pltpu.make_async_copy(count_hbm, count, load_n)
-    load_count.start()
-
     def plane_of(n):
         return (y + nth(n - 1)) % 4
 
@@ -86,6 +81,10 @@
         return pltpu.make_async_copy(tensor_hbm.at[:, columns], tv.at[:, columns], load_t.at[m])
 
     repeat(FIRST, lambda m: load(m).start())
+    load_dens = pltpu.make_async_copy(dens_hbm, dv, load_d)
+    load_dens.start()
+    load_count = pltpu.make_async_copy(count_hbm, count, load_n)
+    load_count.start()
     barrier = pltpu.get_barrier_semaphore()
     to_all(
         lambda a, b: (a, b),

time: 38.1 us -> 38.1 us (level)
  no operation moved by 1% of the time
where the time goes in v5:
time: 38.1 us; the launch traced here: 38 us
  Pallas kernels  36.8 us (97%)
  between operations  0.66 us (2%)
  other arithmetic  0.6 us (2%)
    pallas_call x1, Pallas kernels, body(): pl.pallas_call(kernel, name='coulomb', out_shape=pltpu.VMEM((K // 2, ROWS...  36.8 us

profile of v5, /device:TPU:1, one launch (start us, length us, event | category | flops | bytes accessed | tf_op | source)
XLA Modules:
  0.0 38.0 jit_solution(14584584325663687067)
XLA Ops:
  0.7 36.8 %coulomb.1 = f32[8,768]{1,0:T(8,128)S(1)} custom-call(s32[1]{0:T(128)S(6)} %copy.5.count_hbm, bf16[16,768]{1,0:T(8,128)(2,1)} %dens_hbm.1, bf16[768,10240]{1,0:T(8,128)(2,1)} %tensor_hbm.1, bf16[320,10240]{1,0:T(8,128)(2,1)} %bitcast.1), custom_call_target="tpu_custom_call" | custom-call | tf_op jit(solution)/shard_map/coulomb/pallas_call | solution.py:313
  37.4 0.6 %convert_element_type.3 = bf16[8,768]{1,0:T(8,128)(2,1)} convert(f32[8,768]{1,0:T(8,128)S(1)} %coulomb.1) | non-fusion elementwise | flops 6144 | bytes 36864 | tf_op jit(solution)/shard_map/convert_element_type | solution.py:342
